TPU v7x, 128 devices: a whole 4x4x4 slice. The times are simulated.
128 devices in a mesh: gene: 8 (over y, x_lo), bin: 16 (over z, x_hi, core).
Axes of the slice: x: 4 (x_hi: 2, x_lo: 2; x = x_hi * 2 + x_lo), y: 4, z: 4, core: 2. Of those that a mesh axis runs over, the one named last changes fastest.
Arguments:
- counts: bfloat16 [49152, 18432], P('bin', 'gene'), may hold values from 2 to 80
- factors: float32 [49152, 256], P('bin'), may hold values from 0.01 to 1
- loadings: float32 [256, 18432], P(None, 'gene'), may hold values from 0.01 to 1
- position: int32 [49152], P('bin'), may hold values from 0 to 49151, as said below
- edge_codes: int32 [192, 256], P('bin'), may hold values from 1 to 15
Outputs:
- factors_new: float32 [49152, 256], P('bin')
- loadings_new: float32 [256, 18432], P(None, 'gene')
Inputs may be any that keep to these rules, and one draw needn't show every extreme that they name: Each grid position is named by exactly one barcode. The barcodes of one index s of bin (rows s * 3072 on) fall in 16 aligned groups of 192; group t holds positions in grid rows t * 12 to (t + 1) * 12 - 1, 192 from every such index.
All inputs are finite; a program needn't handle non-finite values.
Results may differ from a plain program's by a relative error of at most 0.0003.
Values sent between devices are 32-bit elements; how exact they have to be, the bound alone decides.
A program may use at most 128 MiB of HBM per device.

v0:
```python
import functools

import jax
import jax.numpy as jnp
from jax import lax
from jax.experimental import pallas as pl
from jax.experimental.pallas import tpu as pltpu
from jax.sharding import PartitionSpec as P

K = 256
G = 18432


def passed_along(block, axis, distance):
    devices = range(lax.axis_size(axis))
    route = [(i - distance, i) for i in devices if i - distance in devices]
    return lax.ppermute(block, axis, route)


def neighbour_sum(values, from_above, from_below):
    upper = jnp.concatenate([from_above[None], values[:-1]], 0)
    lower = jnp.concatenate([values[1:], from_below[None]], 0)
    beside = jnp.pad(values[:, 1:], ((0, 0), (0, 1), (0, 0))) + jnp.pad(
        values[:, :-1], ((0, 0), (1, 0), (0, 0))
    )
    return beside + 0.5 * (lower + upper)


def neighbour_first(values, from_above, from_below):
    upper = jnp.concatenate([from_above[:, None], values[:, :-1]], 1)
    lower = jnp.concatenate([values[:, 1:], from_below[:, None]], 1)
    beside = jnp.pad(values[:, :, 1:], ((0, 0), (0, 0), (0, 1))) + jnp.pad(
        values[:, :, :-1], ((0, 0), (0, 0), (1, 0))
    )
    return beside + 0.5 * (lower + upper)


def gray(value):
    return value + (value // 2) * (1 - 2 * (value % 2))


def gene_at_place(place, count):
    wide = 1 - ((place + count - 1) % count) // (count // 2)
    row = wide * (place - 1) + (1 - wide) * ((count - place) % count)
    return 2 * row + wide


def gene_place(index, count):
    row, wide = index // 2, index % 2
    return wide * (1 + row) + (1 - wide) * ((count - row) % count)


def bin_at_place(place, count):
    plane, step = place // 4, place % 4
    turned = step + (plane % 2) * (3 - 2 * step)
    return plane * 4 + gray(turned)


def bin_place(index, count):
    plane = index // 4
    turned = gray(index % 4)
    return plane * 4 + turned + (plane % 2) * (3 - 2 * turned)


RINGS = {"gene": (gene_at_place, gene_place), "bin": (bin_at_place, bin_place)}


def ring_peers(axis, count):
    at_place, place_of = RINGS[axis]
    place = place_of(lax.axis_index(axis), count)
    return place, (lambda shift: at_place((place + shift + count) % count, count))


def enter(axis, peers):
    barrier = pltpu.get_barrier_semaphore()
    for peer in peers:
        pl.semaphore_signal(barrier, inc=1, device_id={axis: peer},
                            device_id_type=pl.DeviceIdType.MESH)
    pl.semaphore_wait(barrier, len(peers))


def gather_kernel(axis, count, x_ref, out_ref, send_sem, recv_sem):
    place, member = ring_peers(axis, count)
    ahead, behind = member(1), member(-1)
    half = x_ref.shape[0] // 2
    enter(axis, (ahead, behind))
    out_ref[member(0)] = x_ref[...]

    def copy(step, way):
        rows = pl.ds(way * half, half)
        origin = member(-step) if way == 0 else member(step)
        src = x_ref.at[rows] if step == 0 else out_ref.at[origin, rows]
        return pltpu.make_async_remote_copy(
            src_ref=src,
            dst_ref=out_ref.at[origin, rows],
            send_sem=send_sem.at[way, step],
            recv_sem=recv_sem.at[way, step],
            device_id={axis: ahead if way == 0 else behind},
            device_id_type=pl.DeviceIdType.MESH,
        )

    for step in range(count - 1):
        for way in (0, 1):
            if step >= 1:
                copy(step - 1, way).wait_recv()
            copy(step, way).start()
    for way in (0, 1):
        copy(count - 2, way).wait_recv()
    for step in range(count - 1):
        for way in (0, 1):
            copy(step, way).wait_send()


def ring_gather(x, axis, collective_id):
    count = lax.axis_size(axis)
    return pl.pallas_call(
        functools.partial(gather_kernel, axis, count),
        out_shape=jax.ShapeDtypeStruct((count,) + x.shape, x.dtype),
        in_specs=[pl.BlockSpec(memory_space=pltpu.VMEM)],
        out_specs=pl.BlockSpec(memory_space=pltpu.VMEM),
        scratch_shapes=[
            pltpu.SemaphoreType.DMA((2, count - 1)),
            pltpu.SemaphoreType.DMA((2, count - 1)),
        ],
        compiler_params=pltpu.CompilerParams(
            collective_id=collective_id, has_side_effects=True
        ),
    )(x)


def scatter_kernel(axis, count, x_ref, out_ref, got, sent, send_sem, recv_sem):
    place, member = ring_peers(axis, count)
    ahead, behind = member(1), member(-1)
    half = x_ref.shape[2] // 2
    enter(axis, (ahead, behind))

    def copy(step, way):
        lanes = pl.ds(way * half, half)
        if step == 0:
            source = x_ref.at[member(-1) if way == 0 else member(1), :, lanes]
        else:
            source = sent.at[way, step]
        return pltpu.make_async_remote_copy(
            src_ref=source,
            dst_ref=got.at[way, step],
            send_sem=send_sem.at[way, step],
            recv_sem=recv_sem.at[way, step],
            device_id={axis: ahead if way == 0 else behind},
            device_id_type=pl.DeviceIdType.MESH,
        )

    for step in range(count - 1):
        for way in (0, 1):
            if step >= 1:
                lanes = pl.ds(way * half, half)
                owner = member(-step - 1) if way == 0 else member(step + 1)
                copy(step - 1, way).wait_recv()
                sent[way, step] = got[way, step - 1] + x_ref[owner, :, lanes]
            copy(step, way).start()
    for way in (0, 1):
        lanes = pl.ds(way * half, half)
        copy(count - 2, way).wait_recv()
        out_ref[:, lanes] = got[way, count - 2] + x_ref[member(0), :, lanes]
    for step in range(count - 1):
        for way in (0, 1):
            copy(step, way).wait_send()


def ring_scatter(x, axis, collective_id):
    count, rows, lanes = x.shape
    return pl.pallas_call(
        functools.partial(scatter_kernel, axis, count),
        out_shape=jax.ShapeDtypeStruct((rows, lanes), x.dtype),
        in_specs=[pl.BlockSpec(memory_space=pltpu.VMEM)],
        out_specs=pl.BlockSpec(memory_space=pltpu.VMEM),
        scratch_shapes=[
            pltpu.VMEM((2, count - 1, rows, lanes // 2), x.dtype),
            pltpu.VMEM((2, count - 1, rows, lanes // 2), x.dtype),
            pltpu.SemaphoreType.DMA((2, count - 1)),
            pltpu.SemaphoreType.DMA((2, count - 1)),
        ],
        compiler_params=pltpu.CompilerParams(
            collective_id=collective_id, has_side_effects=True
        ),
    )(x)


def greet_all(axis, me, count):
    barrier = pltpu.get_barrier_semaphore()
    for shift in range(1, count):
        pl.semaphore_signal(barrier, inc=1, device_id={axis: (me + shift) % count},
                            device_id_type=pl.DeviceIdType.MESH)
    pl.semaphore_wait(barrier, count - 1)


def exchange_kernel(axis, count, summed, x_ref, out_ref, *rest):
    if summed:
        got, send_sem, recv_sem = rest
    else:
        got, (send_sem, recv_sem) = out_ref, rest
    me = lax.axis_index(axis)
    greet_all(axis, me, count)

    def copy(shift):
        target = (me + shift) % count
        return pltpu.make_async_remote_copy(
            src_ref=x_ref.at[target] if summed else x_ref,
            dst_ref=got.at[me],
            send_sem=send_sem.at[shift],
            recv_sem=recv_sem.at[me],
            device_id={axis: target},
            device_id_type=pl.DeviceIdType.MESH,
        )

    def arrival(shift):
        origin = (me + count - shift) % count
        return pltpu.make_async_remote_copy(
            src_ref=x_ref.at[origin] if summed else x_ref,
            dst_ref=got.at[origin],
            send_sem=send_sem.at[shift],
            recv_sem=recv_sem.at[origin],
            device_id={axis: origin},
            device_id_type=pl.DeviceIdType.MESH,
        )

    for shift in range(1, count):
        copy(shift).start()
    if summed:
        total = x_ref[me]
        for shift in range(1, count):
            arrival(shift).wait_recv()
            total = total + got[(me + count - shift) % count]
        out_ref[...] = total
    else:
        out_ref[me] = x_ref[...]
        for shift in range(1, count):
            arrival(shift).wait_recv()
    for shift in range(1, count):
        copy(shift).wait_send()


def exchange(x, axis, collective_id, summed):
    count = lax.axis_size(axis)
    if summed:
        out_shape = x.shape[1:]
        scratch = [pltpu.VMEM(x.shape, x.dtype)]
    else:
        out_shape = (count,) + x.shape
        scratch = []
    return pl.pallas_call(
        functools.partial(exchange_kernel, axis, count, summed),
        out_shape=jax.ShapeDtypeStruct(out_shape, x.dtype),
        in_specs=[pl.BlockSpec(memory_space=pltpu.VMEM)],
        out_specs=pl.BlockSpec(memory_space=pltpu.VMEM),
        scratch_shapes=scratch + [
            pltpu.SemaphoreType.DMA((count,)),
            pltpu.SemaphoreType.DMA((count,)),
        ],
        compiler_params=pltpu.CompilerParams(
            collective_id=collective_id, has_side_effects=True
        ),
    )(x)


def factor_gather_kernel(count, x_ref, out_ref, half_ref, send_sem, recv_sem):
    me = lax.axis_index("gene")
    greet_all("gene", me, count)

    def copy(shift, index, peer):
        return pltpu.make_async_remote_copy(
            src_ref=x_ref,
            dst_ref=out_ref.at[index],
            send_sem=send_sem.at[shift],
            recv_sem=recv_sem.at[index],
            device_id={"gene": peer},
            device_id_type=pl.DeviceIdType.MESH,
        )

    for shift in range(1, count):
        copy(shift, me, (me + shift) % count).start()
    out_ref[me] = x_ref[...]
    for shift in range(1, count):
        origin = (me + count - shift) % count
        copy(shift, origin, origin).wait_recv()
    half_ref[...] = out_ref[...].astype(half_ref.dtype)
    for shift in range(1, count):
        copy(shift, me, (me + shift) % count).wait_send()


def factor_gather(x, collective_id):
    count = lax.axis_size("gene")
    vmem = pl.BlockSpec(memory_space=pltpu.VMEM)
    shape = (count,) + x.shape
    return pl.pallas_call(
        functools.partial(factor_gather_kernel, count),
        out_shape=(
            jax.ShapeDtypeStruct(shape, x.dtype),
            jax.ShapeDtypeStruct(shape, jnp.bfloat16),
        ),
        in_specs=[vmem],
        out_specs=(vmem, vmem),
        scratch_shapes=[pltpu.SemaphoreType.DMA((count,))] * 2,
        compiler_params=pltpu.CompilerParams(
            collective_id=collective_id, has_side_effects=True
        ),
    )(x)


def loadings_kernel(count, cross_ref, gram_ref, load_ref, out_ref, got, got_gram, sem_a, sem_b, sem_c, sem_d):
    me = lax.axis_index("bin")
    greet_all("bin", me, count)

    def remote(src, dst, send, recv, shift, index, peer):
        return pltpu.make_async_remote_copy(
            src_ref=src.at[index],
            dst_ref=dst.at[index],
            send_sem=send.at[shift],
            recv_sem=recv.at[index],
            device_id={"bin": peer},
            device_id_type=pl.DeviceIdType.MESH,
        )

    def partial_copies(shift):
        target = (me + shift) % count
        return (
            pltpu.make_async_remote_copy(
                src_ref=cross_ref.at[target], dst_ref=got.at[me], send_sem=sem_a.at[0, shift],
                recv_sem=sem_b.at[0, me], device_id={"bin": target},
                device_id_type=pl.DeviceIdType.MESH,
            ),
            pltpu.make_async_remote_copy(
                src_ref=gram_ref.at[target], dst_ref=got_gram.at[me], send_sem=sem_a.at[1, shift],
                recv_sem=sem_b.at[1, me], device_id={"bin": target},
                device_id_type=pl.DeviceIdType.MESH,
            ),
        )

    def partial_arrivals(shift):
        origin = (me + count - shift) % count
        return (
            pltpu.make_async_remote_copy(
                src_ref=cross_ref.at[origin], dst_ref=got.at[origin], send_sem=sem_a.at[0, shift],
                recv_sem=sem_b.at[0, origin], device_id={"bin": origin},
                device_id_type=pl.DeviceIdType.MESH,
            ),
            pltpu.make_async_remote_copy(
                src_ref=gram_ref.at[origin], dst_ref=got_gram.at[origin], send_sem=sem_a.at[1, shift],
                recv_sem=sem_b.at[1, origin], device_id={"bin": origin},
                device_id_type=pl.DeviceIdType.MESH,
            ),
        )

    def result_copy(shift):
        target = (me + shift) % count
        return remote(out_ref, out_ref, sem_c, sem_d, shift, me, target)

    def result_arrival(shift):
        origin = (me + count - shift) % count
        return remote(out_ref, out_ref, sem_c, sem_d, shift, origin, origin)

    for shift in range(1, count):
        for copy in partial_copies(shift):
            copy.start()
    cross = cross_ref[me]
    fac_gram = gram_ref[me]
    for shift in range(1, count):
        origin = (me + count - shift) % count
        for copy in partial_arrivals(shift):
            copy.wait_recv()
        cross = cross + got[origin]
        fac_gram = fac_gram + got_gram[origin]
    rows = cross.shape[0]
    own = load_ref[pl.ds(pl.multiple_of(me * rows, rows), rows), :]
    denom = jnp.dot(
        fac_gram, load_ref[...], precision=lax.Precision.HIGHEST,
        preferred_element_type=jnp.float32,
    )
    out_ref[me] = own * cross / denom
    for shift in range(1, count):
        for copy in partial_copies(shift):
            copy.wait_send()
    for shift in range(1, count):
        result_copy(shift).start()
    for shift in range(1, count):
        result_arrival(shift).wait_recv()
    for shift in range(1, count):
        result_copy(shift).wait_send()


def loadings_update(cross_parts, gram_parts, loadings, collective_id):
    count, rows, genes = cross_parts.shape
    vmem = pl.BlockSpec(memory_space=pltpu.VMEM)
    return pl.pallas_call(
        functools.partial(loadings_kernel, count),
        out_shape=jax.ShapeDtypeStruct((count, rows, genes), loadings.dtype),
        in_specs=[vmem, vmem, vmem],
        out_specs=vmem,
        scratch_shapes=[
            pltpu.VMEM(cross_parts.shape, cross_parts.dtype),
            pltpu.VMEM(gram_parts.shape, gram_parts.dtype),
            pltpu.SemaphoreType.DMA((2, count)),
            pltpu.SemaphoreType.DMA((2, count)),
            pltpu.SemaphoreType.DMA((count,)),
            pltpu.SemaphoreType.DMA((count,)),
        ],
        compiler_params=pltpu.CompilerParams(
            collective_id=collective_id, has_side_effects=True
        ),
    )(cross_parts, gram_parts, loadings)


def split_three(values):
    high = lax.reduce_precision(values, exponent_bits=8, mantissa_bits=7)
    rest = values - high
    mid = lax.reduce_precision(rest, exponent_bits=8, mantissa_bits=7)
    low = rest - mid
    return jnp.concatenate([high, mid, low], 1).astype(jnp.bfloat16)


def join_three(parts, width):
    return (parts[:, :width] + parts[:, width : 2 * width]) + parts[:, 2 * width :]


def stencil_term(own, position, edge_codes):
    bin_count = lax.axis_size("bin")
    row_count, width = own.shape
    group_size = row_count // bin_count
    grid_rows, grid_cols = edge_codes.shape
    payload = jnp.concatenate([own, position.astype(jnp.float32)[:, None]], 1)
    got = lax.all_to_all(
        payload.reshape(bin_count, group_size * (width + 1)), "bin", 0, 0, tiled=True
    ).reshape(row_count, width + 1)
    tile_slot = got[:, width].astype(jnp.int32) - lax.axis_index("bin") * row_count
    cells = lax.broadcasted_iota(jnp.int32, (row_count, row_count), 1)
    onehot = (tile_slot[:, None] == cells).astype(jnp.bfloat16)
    placed = lax.dot_general(
        onehot, split_three(got[:, :width]), (((0,), (0,)), ((), ())),
        preferred_element_type=jnp.float32,
    )
    tile_rows = join_three(placed, width)
    cell_scale = edge_codes.astype(jnp.float32) / 8.0
    weighted = cell_scale[:, :, None] * tile_rows.reshape(grid_rows, grid_cols, width)
    rim_last, rim_first = (weighted[-1], weighted[0])
    upper_rows, upper_scale = passed_along((rim_last, cell_scale[-1]), "bin", 1)
    lower_rows, lower_scale = passed_along((rim_first, cell_scale[0]), "bin", -1)
    degree_grid = (
        cell_scale * neighbour_first(cell_scale[None], upper_scale[None], lower_scale[None])[0]
    )
    smooth_grid = cell_scale[:, :, None] * neighbour_sum(weighted, upper_rows, lower_rows)
    back = jnp.concatenate(
        [smooth_grid.reshape(row_count, width), degree_grid.reshape(row_count, 1)], 1
    )
    back_rows = join_three(
        jnp.dot(onehot, split_three(back), preferred_element_type=jnp.float32), width + 1
    )
    ret = lax.all_to_all(
        back_rows.reshape(bin_count, group_size * (width + 1)), "bin", 0, 0, tiled=True
    ).reshape(row_count, width + 1)
    return (ret[:, :width], ret[:, width])


def on_device(counts, factors, loadings, position, edge_codes):
    bin_count = lax.axis_size("bin")
    gene_count = lax.axis_size("gene")
    row_count, width_all = factors.shape
    width = width_all // gene_count
    k_rows = width_all // bin_count
    gene_at = lax.axis_index("gene")
    bin_at = lax.axis_index("bin")
    load_bf = loadings.astype(jnp.bfloat16)
    right_dims = (((1,), (1,)), ((), ()))
    numer_part = lax.dot_general(load_bf, counts, right_dims, preferred_element_type=jnp.float32)
    gram_part = lax.dot_general(load_bf, load_bf, right_dims, preferred_element_type=jnp.float32)
    both = jnp.concatenate([numer_part, gram_part], 1)
    both = lax.psum_scatter(
        both.reshape(gene_count, width, -1), "gene", scatter_dimension=0, tiled=True
    ).reshape(width, -1)
    numer_t, gram_rows = both[:, :row_count], both[:, row_count:]
    own = lax.dynamic_slice_in_dim(factors, gene_at * width, width, 1)
    smooth, degree = stencil_term(own, position, edge_codes)
    penalty = float(G * K) / 64.0
    own_t = own.T
    denom_t = (
        lax.dot_general(gram_rows, factors, right_dims, precision=lax.Precision.HIGHEST)
        + penalty * degree[None, :] * own_t
    )
    new_t = own_t * (numer_t + penalty * smooth.T) / denom_t
    factors_t, fac_bf_t = factor_gather(new_t, 0)
    factors_new = factors_t.reshape(width_all, row_count).T
    fac_bf_t = fac_bf_t.reshape(width_all, row_count)
    cross_part = jnp.dot(fac_bf_t, counts, preferred_element_type=jnp.float32)
    fgram_part = lax.dot_general(fac_bf_t, fac_bf_t, right_dims, preferred_element_type=jnp.float32)
    loadings_new = loadings_update(
        cross_part.reshape(bin_count, k_rows, -1),
        fgram_part.reshape(bin_count, k_rows, -1),
        loadings,
        2,
    ).reshape(width_all, -1)
    return (factors_new, loadings_new)


def solution(mesh):
    placed = (P("bin", "gene"), P("bin", None), P(None, "gene"), P("bin"), P("bin", None))
    return jax.shard_map(
        on_device,
        mesh=mesh,
        in_specs=placed,
        out_specs=(P("bin", None), P(None, "gene")),
        check_vma=False,
    )
```

profile of v0, /device:TPU:1, one launch (start us, length us, event | category | flops | bytes accessed | tf_op | source)
XLA Modules:
  0.0 287.9 jit_solution(17902327558767403272)
XLA Ops:
  7.2 0.0 copy-start
  7.2 0.9 fusion.38
  8.1 0.6 copy-done.4
  8.6 0.6 fusion.43
  9.2 3.3 %collective-permute-start.2 = (f32[256]{0:T(256)}, f32[256]{0:T(256)}, u32[]{:S(2)}, u32[]{:S(2)}) collective-permute-start(f32[256]{0:T(256)} %bitcast.7), channel_id=1, source_target_pairs={{1,0},{2,1},{3,2},{4,3},{5,4},{6,5},{7,6},{8,7},{9,8},{10,9},{11,1... | collective-permute-start | bytes 3080 | tf_op jit(solution)/shard_map/ppermute | solution.py:17
  12.6 4.6 %collective-permute-start.3 = (f32[256]{0:T(256)}, f32[256]{0:T(256)}, u32[]{:S(2)}, u32[]{:S(2)}) collective-permute-start(f32[256]{0:T(256)} %bitcast.9), channel_id=1, source_target_pairs={{0,1},{1,2},{2,3},{3,4},{4,5},{5,6},{6,7},{7,8},{8,9},{9,10},{10,1... | collective-permute-start | bytes 3080 | tf_op jit(solution)/shard_map/ppermute | solution.py:17
  17.2 1.3 convert_element_type.25
  18.5 1.6 constant_dynamic-slice_fusion
  20.1 1.8 copy.50
  22.0 1.5 pad_maximum_fusion.1
  23.5 2.7 copy.40
  26.2 3.9 %all_to_all.16 = f32[16,1,6336]{2,1,0:T(1,128)} reshape(f32[3072,33]{1,0:T(8,128)} %copy.40) | data formatting | bytes 811008 | tf_op jit(solution)/shard_map/all_to_all | solution.py:430
  30.0 8.6 %all-to-all-start = ((f32[16,1,6336]{2,1,0:T(1,128)}), f32[16,1,6336]{2,1,0:T(1,128)}, u32[]{:S(2)}, u32[]{:S(2)}) async-start(f32[16,1,6336]{2,1,0:T(1,128)} %all_to_all.16), calls=%async_computation.1 | async-start | bytes 819200 | tf_op jit(solution)/shard_map/all_to_all | solution.py:430
  38.6 0.5 reduce-scatter.2.cloned.1.call-start
  39.1 0.0 copy-start.1
  39.1 3.0 %fusion.20 = f32[256,256]{1,0:T(8,128)S(1)} fusion(f32[256,2304]{1,0:T(8,128)} %load_ref.1), kind=kOutput, calls=%fused_computation.29 | convolution fusion | flops 302579712 | bytes 2621440 | tf_op jit(solution)/shard_map/dot_general | solution.py:473
  42.2 0.0 copy-done.1
  42.2 10.7 %fusion.22 = f32[256,3072]{1,0:T(8,128)} fusion(bf16[3072,2304]{1,0:T(8,128)(2,1)} %param.5, f32[256,2304]{1,0:T(8,128)S(1)} %copy-done.1), kind=kOutput, calls=%fused_computation.31 | convolution fusion | flops 3624468480 | bytes 19660800 | tf_op jit(solution)/shard_map/dot_general | solution.py:472
  52.9 3.9 %pad_maximum_fusion = f32[256,3328]{1,0:T(8,128)} fusion(f32[256,256]{1,0:T(8,128)S(1)} %fusion.20, f32[256,3072]{1,0:T(8,128)} %fusion.22), kind=kLoop, calls=%fused_computation.9 | loop fusion | flops 851968 | bytes 6815744 | tf_op jit(solution)/shard_map/concatenate | solution.py:474
  56.7 0.0 reduce-scatter.2.cloned.1.call-update
  56.7 0.6 fusion.44
  57.4 0.7 fusion.42
  58.0 0.0 collective-permute-done.2
  58.0 0.0 collective-permute-done.3
  58.0 0.9 fusion.35
  58.9 0.6 copy.56
  59.5 0.0 all-to-all-done
  59.5 2.7 reduce
  62.3 4.0 %reshape.126 = f32[3072,33]{1,0:T(8,128)} reshape(f32[16,6336]{1,0:T(8,128)} %reduce) | data formatting | bytes 811008 | tf_op jit(solution)/shard_map/reshape | solution.py:432
  66.2 2.8 copy.51
  69.1 2.4 fusion.9
  71.4 0.1 reduce-precision_convert_fusion.3
  71.5 7.7 %fusion.1 = f32[3072,96]{0,1:T(8,128)S(1)} fusion(s32[3072]{0:T(1024)S(1)} %fusion.9, bf16[3072,32]{0,1:T(8,128)(2,1)S(1)} %get-tuple-element.16, bf16[3072,32]{0,1:T(8,128)(2,1)S(1)} %get-tuple-element.17, bf16[3072,32]{0,1:T(8,128)(2,1)S(1)} %get-tuple-element.15), kind=kOutput, calls=%fused_computation.2 | convolution fusion | flops 1823145984 | bytes 1781760 | tf_op jit(solution)/shard_map/dot_general | solution.py:436
  79.3 0.8 slice_add_fusion.2
  80.1 1.9 reshape.127
  82.0 1.1 broadcast_multiply_fusion
  83.1 2.0 collective-permute-start
  85.2 5.0 %collective-permute-start.1 = (f32[256,32]{0,1:T(8,128)S(1)}, f32[256,32]{0,1:T(8,128)S(1)}, u32[]{:S(2)}, u32[]{:S(2)}) collective-permute-start(f32[256,32]{0,1:T(8,128)S(1)} %bitcast.73), channel_id=1, source_target_pairs={{0,1},{1,2},{2,3},{3,4},{4,5},{5,6},{6,7},{7,8},{8,9},{9,10},{10,1... | collective-permute-start | bytes 98312 | tf_op jit(solution)/shard_map/ppermute | solution.py:17
  90.2 0.1 fusion.41
  90.3 0.2 fusion.39
  90.5 0.2 collective-permute-done
  90.8 1.2 collective-permute-done.1
  92.0 0.3 fusion.26
  92.3 0.2 copy.55
  92.5 0.8 constant_dynamic-update-slice_fusion
  93.3 1.6 dynamic-update-slice.1
  94.9 1.1 reduce-precision_convert_fusion.1
  96.0 8.8 %fusion = f32[3072,99]{0,1:T(8,128)S(1)} fusion(s32[3072]{0:T(1024)} %copy-done.7, bf16[3072,33]{0,1:T(8,128)(2,1)S(1)} %get-tuple-element.13, bf16[3072,33]{0,1:T(8,128)(2,1)S(1)} %get-tuple-element.14, bf16[3072,33]{0,1:T(8,128)(2,1)S(1)} %get-tuple-element.12), kind=kOutput, calls=%fused_computation.1 | convolution fusion | flops 1879824384 | bytes 1837056 | tf_op jit(solution)/shard_map/dot_general | solution.py:454
  104.8 0.9 slice_add_fusion
  105.7 2.7 copy.45
  108.3 3.8 %all_to_all.17 = f32[16,1,6336]{2,1,0:T(1,128)} reshape(f32[3072,33]{1,0:T(8,128)} %copy.45) | data formatting | bytes 811008 | tf_op jit(solution)/shard_map/all_to_all | solution.py:456
  112.2 24.8 %all_to_all.20 = f32[16,1,6336]{2,1,0:T(1,128)} all-to-all(f32[16,1,6336]{2,1,0:T(1,128)} %all_to_all.17), channel_id=1, replica_groups=mesh['gene'=8,'bin'=16] {'bin'}, dimensions={0} | all-to-all | bytes 811008 | tf_op jit(solution)/shard_map/all_to_all | solution.py:456
  137.0 2.7 reduce.2
  139.7 4.0 %reshape.130 = f32[3072,33]{1,0:T(8,128)} reshape(f32[16,6336]{1,0:T(8,128)} %reduce.2) | data formatting | bytes 811008 | tf_op jit(solution)/shard_map/reshape | solution.py:458
  143.7 2.6 copy.54
  146.3 2.3 fusion.7
  148.6 0.0 reduce-scatter.2.cloned.1.call-done
  148.6 4.8 %fusion.6.x_ref = f32[32,3072]{1,0:T(8,128)} fusion(f32[3072,256]{1,0:T(8,128)S(1)} %copy-done, f32[32,3328]{1,0:T(8,128)} %bitcast.75, f32[3072,32]{0,1:T(8,128)S(1)} %copy.50, f32[3072,32]{0,1:T(8,128)} %copy.54, f32[3072]{0:T(1024)S(1)} %fusion.7), kind=kOutput, calls=%fused_computation.8 | convolution fusion | flops 302579712 | bytes 4763648 | tf_op jit(solution)/shard_map/dot_general | solution.py:484
  153.4 41.5 %shard_map.68 = (f32[8,32,3072]{2,1,0:T(8,128)}, bf16[8,32,3072]{2,1,0:T(8,128)(2,1)}) custom-call(f32[32,3072]{1,0:T(8,128)} %fusion.6.x_ref), custom_call_target="tpu_custom_call" | custom-call | tf_op jit(solution)/shard_map/pallas_call | solution.py:294
  194.9 3.5 %copy.48 = f32[256,3072]{0,1:T(8,128)} copy(f32[256,3072]{1,0:T(8,128)} %bitcast.68) | data formatting | bytes 6291456 | tf_op jit(solution)/shard_map/reshape | solution.py:489
  198.4 10.8 %fusion.4.cross_ref = f32[16,16,2304]{2,1,0:T(8,128)} fusion(bf16[16,16,3072]{2,1,0:T(8,128)(2,1)} %bitcast.64, bf16[3072,2304]{1,0:T(8,128)(2,1)} %param.5), kind=kOutput, calls=%fused_computation.5 | convolution fusion | flops 3623878656 | bytes 18087936 | tf_op jit(solution)/shard_map/dot_general | solution.py:491
  209.3 1.3 fusion.45.gram_ref
  210.6 67.0 %shard_map.69 = f32[16,16,2304]{2,1,0:T(8,128)} custom-call(f32[16,16,2304]{2,1,0:T(8,128)} %fusion.4.cross_ref, f32[16,16,256]{2,1,0:T(8,128)} %fusion.45.gram_ref, f32[256,2304]{1,0:T(8,128)} %load_ref.1), custom_call_target="tpu_custom_call" | custom-call | tf_op jit(solution)/shard_map/pallas_call | solution.py:393
  277.6 3.2 %copy.63 = f32[256,2304]{1,0:T(8,128)} copy(f32[256,2304]{1,0:T(8,128)} %bitcast.63) | data formatting | bytes 4718592
  (17 shorter events, 0.1 us)
Async XLA Ops:
  7.2 11.4 %copy-start = (f32[3072,256]{1,0:T(8,128)S(1)}, f32[3072,256]{1,0:T(8,128)}, u32[]{:S(2)}) copy-start(f32[3072,256]{1,0:T(8,128)} %param.6) | copy-start | bytes 9437188
  8.1 0.6 copy-start.4
  9.2 48.8 %collective-permute-start.2 = (f32[256]{0:T(256)}, f32[256]{0:T(256)}, u32[]{:S(2)}, u32[]{:S(2)}) collective-permute-start(f32[256]{0:T(256)} %bitcast.7), channel_id=1, source_target_pairs={{1,0},{2,1},{3,2},{4,3},{5,4},{6,5},{7,6},{8,7},{9,8},{10,9},{11,1... | collective-permute-start | bytes 3080 | tf_op jit(solution)/shard_map/ppermute | solution.py:17
  12.6 45.5 %collective-permute-start.3 = (f32[256]{0:T(256)}, f32[256]{0:T(256)}, u32[]{:S(2)}, u32[]{:S(2)}) collective-permute-start(f32[256]{0:T(256)} %bitcast.9), channel_id=1, source_target_pairs={{0,1},{1,2},{2,3},{3,4},{4,5},{5,6},{6,7},{7,8},{8,9},{9,10},{10,1... | collective-permute-start | bytes 3080 | tf_op jit(solution)/shard_map/ppermute | solution.py:17
  30.0 29.5 %all-to-all-start = ((f32[16,1,6336]{2,1,0:T(1,128)}), f32[16,1,6336]{2,1,0:T(1,128)}, u32[]{:S(2)}, u32[]{:S(2)}) async-start(f32[16,1,6336]{2,1,0:T(1,128)} %all_to_all.16), calls=%async_computation.1 | async-start | bytes 819200 | tf_op jit(solution)/shard_map/all_to_all | solution.py:430
  38.6 110.0 %reduce-scatter.2.cloned.1.call-start = ((), (), s32[]{:S(2)}) async-start(), calls=%async_computation.3 | async-start | bytes 3833856 | tf_op jit(solution)/shard_map/reduce_scatter | solution.py:475
  39.1 3.1 %copy-start.1 = (f32[256,2304]{1,0:T(8,128)S(1)}, f32[256,2304]{1,0:T(8,128)}, u32[]{:S(2)}) copy-start(f32[256,2304]{1,0:T(8,128)} %load_ref.1) | copy-start | bytes 7077892
  69.1 2.4 copy-start.3
  71.4 7.8 %copy-start.7 = (s32[3072]{0:T(1024)}, s32[3072]{0:T(1024)S(1)}, u32[]{:S(2)}) copy-start(s32[3072]{0:T(1024)S(1)} %fusion.9) | copy-start | bytes 36868
  79.3 2.7 copy-start.5
  83.1 7.6 %collective-permute-start = (f32[256,32]{0,1:T(8,128)S(1)}, f32[256,32]{0,1:T(8,128)S(1)}, u32[]{:S(2)}, u32[]{:S(2)}) collective-permute-start(f32[256,32]{0,1:T(8,128)S(1)} %bitcast.74), channel_id=1, source_target_pairs={{1,0},{2,1},{3,2},{4,3},{5,4},{6,5},{7,6},{8,7},{9,8},{10,9},{11,1... | collective-permute-start | bytes 98312 | tf_op jit(solution)/shard_map/ppermute | solution.py:17
  85.2 6.7 %collective-permute-start.1 = (f32[256,32]{0,1:T(8,128)S(1)}, f32[256,32]{0,1:T(8,128)S(1)}, u32[]{:S(2)}, u32[]{:S(2)}) collective-permute-start(f32[256,32]{0,1:T(8,128)S(1)} %bitcast.73), channel_id=1, source_target_pairs={{0,1},{1,2},{2,3},{3,4},{4,5},{5,6},{6,7},{7,8},{8,9},{9,10},{10,1... | collective-permute-start | bytes 98312 | tf_op jit(solution)/shard_map/ppermute | solution.py:17
  92.3 1.0 copy-start.6
  198.4 10.8 %copy-start.2 = (bf16[8,32,3072]{2,1,0:T(8,128)(2,1)S(1)}, bf16[8,32,3072]{2,1,0:T(8,128)(2,1)}, u32[]{:S(2)}) copy-start(bf16[8,32,3072]{2,1,0:T(8,128)(2,1)} %get-tuple-element.5) | copy-start | bytes 4718596
Sparse Core Ops, SparseCore 0:
  56.9 82.3 reduce-scatter.1
where the time goes:
time: 292 us; the launch traced here: 288 us
  Pallas kernels  108 us (37%)
  matrix products  47.1 us (16%)
  local copies, waits for them, and re-layouts  44.6 us (15%)
  blocking collectives  24.8 us (8%)
  starting transfers between devices  24.1 us (8%)
  other arithmetic  22.9 us (8%)
  between operations  14.5 us (5%)
    pallas_call x1, Pallas kernels, loadings_update(): pl.pallas_call(functools.partial(loadings_kernel, count), out_shape=jax.S...  67 us
    pallas_call x1, Pallas kernels, factor_gather(): pl.pallas_call(functools.partial(factor_gather_kernel, count), out_shape=...  41.5 us
    all_to_all x1, blocking collectives, stencil_term(): lax.all_to_all(back_rows.reshape(bin_count, group_size * (width + 1)), 'b...  24.8 us
    ppermute x4, starting transfers between devices, passed_along(): return lax.ppermute(block, axis, route)  15 us
    unnamed x25, local copies, waits for them, and re-layouts  12.8 us
    dot_general x1, matrix products, on_device(): cross_part = jnp.dot(fac_bf_t, counts, preferred_element_type=jnp.float32)  10.8 us
    dot_general x1, matrix products, on_device(): lax.dot_general(load_bf, counts, right_dims, preferred_element_type=jnp.f...  10.7 us
    dot_general x1, matrix products, stencil_term(): jnp.dot(onehot, split_three(back), preferred_element_type=jnp.float32)  8.77 us
  transfers between devices with their start and end apart: 6, of which 2 were waited for; matrix products, arithmetic and copies ran while one was open for 28% of the time, Pallas kernels for 0%

commit v1 on v0

--- a/solution.py
+++ b/solution.py
@@ -377,10 +377,10 @@
     )
     out_ref[me] = own * cross / denom
     for shift in range(1, count):
+        result_copy(shift).start()
+    for shift in range(1, count):
         for copy in partial_copies(shift):
             copy.wait_send()
-    for shift in range(1, count):
-        result_copy(shift).start()
     for shift in range(1, count):
         result_arrival(shift).wait_recv()
     for shift in range(1, count):

time: 292 us -> 292 us (level)
  no operation moved by 1% of the time
where the time goes in v1:
time: 292 us; the launch traced here: 288 us
  Pallas kernels  108 us (37%)
  matrix products  47.1 us (16%)
  local copies, waits for them, and re-layouts  44.6 us (15%)
  blocking collectives  24.8 us (8%)
  starting transfers between devices  24.1 us (8%)
  other arithmetic  22.9 us (8%)
  between operations  14.5 us (5%)
    pallas_call x1, Pallas kernels, loadings_update(): pl.pallas_call(functools.partial(loadings_kernel, count), out_shape=jax.S...  66.9 us
    pallas_call x1, Pallas kernels, factor_gather(): pl.pallas_call(functools.partial(factor_gather_kernel, count), out_shape=...  41.5 us
    all_to_all x1, blocking collectives, stencil_term(): lax.all_to_all(back_rows.reshape(bin_count, group_size * (width + 1)), 'b...  24.8 us
    ppermute x4, starting transfers between devices, passed_along(): return lax.ppermute(block, axis, route)  15 us
    unnamed x25, local copies, waits for them, and re-layouts  12.8 us
    dot_general x1, matrix products, on_device(): cross_part = jnp.dot(fac_bf_t, counts, preferred_element_type=jnp.float32)  10.8 us
    dot_general x1, matrix products, on_device(): lax.dot_general(load_bf, counts, right_dims, preferred_element_type=jnp.f...  10.7 us
    dot_general x1, matrix products, stencil_term(): jnp.dot(onehot, split_three(back), preferred_element_type=jnp.float32)  8.77 us
  transfers between devices with their start and end apart: 6, of which 2 were waited for; matrix products, arithmetic and copies ran while one was open for 28% of the time, Pallas kernels for 0%

profile of v1, /device:TPU:1, one launch (start us, length us, event | category | flops | bytes accessed | tf_op | source)
XLA Modules:
  0.0 287.8 jit_solution(7396454141025074666)
XLA Ops:
  7.2 0.0 copy-start
  7.2 0.9 fusion.38
  8.1 0.6 copy-done.4
  8.6 0.6 fusion.43
  9.2 3.3 %collective-permute-start.2 = (f32[256]{0:T(256)}, f32[256]{0:T(256)}, u32[]{:S(2)}, u32[]{:S(2)}) collective-permute-start(f32[256]{0:T(256)} %bitcast.7), channel_id=1, source_target_pairs={{1,0},{2,1},{3,2},{4,3},{5,4},{6,5},{7,6},{8,7},{9,8},{10,9},{11,1... | collective-permute-start | bytes 3080 | tf_op jit(solution)/shard_map/ppermute | solution.py:17
  12.6 4.6 %collective-permute-start.3 = (f32[256]{0:T(256)}, f32[256]{0:T(256)}, u32[]{:S(2)}, u32[]{:S(2)}) collective-permute-start(f32[256]{0:T(256)} %bitcast.9), channel_id=1, source_target_pairs={{0,1},{1,2},{2,3},{3,4},{4,5},{5,6},{6,7},{7,8},{8,9},{9,10},{10,1... | collective-permute-start | bytes 3080 | tf_op jit(solution)/shard_map/ppermute | solution.py:17
  17.2 1.3 convert_element_type.25
  18.5 1.6 constant_dynamic-slice_fusion
  20.1 1.8 copy.50
  22.0 1.5 pad_maximum_fusion.1
  23.5 2.7 copy.40
  26.2 3.9 %all_to_all.16 = f32[16,1,6336]{2,1,0:T(1,128)} reshape(f32[3072,33]{1,0:T(8,128)} %copy.40) | data formatting | bytes 811008 | tf_op jit(solution)/shard_map/all_to_all | solution.py:430
  30.0 8.6 %all-to-all-start = ((f32[16,1,6336]{2,1,0:T(1,128)}), f32[16,1,6336]{2,1,0:T(1,128)}, u32[]{:S(2)}, u32[]{:S(2)}) async-start(f32[16,1,6336]{2,1,0:T(1,128)} %all_to_all.16), calls=%async_computation.1 | async-start | bytes 819200 | tf_op jit(solution)/shard_map/all_to_all | solution.py:430
  38.6 0.5 reduce-scatter.2.cloned.1.call-start
  39.1 0.0 copy-start.1
  39.1 3.0 %fusion.20 = f32[256,256]{1,0:T(8,128)S(1)} fusion(f32[256,2304]{1,0:T(8,128)} %load_ref.1), kind=kOutput, calls=%fused_computation.29 | convolution fusion | flops 302579712 | bytes 2621440 | tf_op jit(solution)/shard_map/dot_general | solution.py:473
  42.2 0.0 copy-done.1
  42.2 10.7 %fusion.22 = f32[256,3072]{1,0:T(8,128)} fusion(bf16[3072,2304]{1,0:T(8,128)(2,1)} %param.5, f32[256,2304]{1,0:T(8,128)S(1)} %copy-done.1), kind=kOutput, calls=%fused_computation.31 | convolution fusion | flops 3624468480 | bytes 19660800 | tf_op jit(solution)/shard_map/dot_general | solution.py:472
  52.9 3.9 %pad_maximum_fusion = f32[256,3328]{1,0:T(8,128)} fusion(f32[256,256]{1,0:T(8,128)S(1)} %fusion.20, f32[256,3072]{1,0:T(8,128)} %fusion.22), kind=kLoop, calls=%fused_computation.9 | loop fusion | flops 851968 | bytes 6815744 | tf_op jit(solution)/shard_map/concatenate | solution.py:474
  56.7 0.0 reduce-scatter.2.cloned.1.call-update
  56.7 0.6 fusion.44
  57.4 0.7 fusion.42
  58.0 0.0 collective-permute-done.2
  58.0 0.0 collective-permute-done.3
  58.0 0.9 fusion.35
  58.9 0.6 copy.56
  59.5 0.0 all-to-all-done
  59.5 2.7 reduce
  62.3 4.0 %reshape.126 = f32[3072,33]{1,0:T(8,128)} reshape(f32[16,6336]{1,0:T(8,128)} %reduce) | data formatting | bytes 811008 | tf_op jit(solution)/shard_map/reshape | solution.py:432
  66.2 2.8 copy.51
  69.1 2.4 fusion.9
  71.4 0.1 reduce-precision_convert_fusion.3
  71.5 7.7 %fusion.1 = f32[3072,96]{0,1:T(8,128)S(1)} fusion(s32[3072]{0:T(1024)S(1)} %fusion.9, bf16[3072,32]{0,1:T(8,128)(2,1)S(1)} %get-tuple-element.16, bf16[3072,32]{0,1:T(8,128)(2,1)S(1)} %get-tuple-element.17, bf16[3072,32]{0,1:T(8,128)(2,1)S(1)} %get-tuple-element.15), kind=kOutput, calls=%fused_computation.2 | convolution fusion | flops 1823145984 | bytes 1781760 | tf_op jit(solution)/shard_map/dot_general | solution.py:436
  79.3 0.8 slice_add_fusion.2
  80.1 1.9 reshape.127
  82.0 1.1 broadcast_multiply_fusion
  83.1 2.0 collective-permute-start
  85.2 5.0 %collective-permute-start.1 = (f32[256,32]{0,1:T(8,128)S(1)}, f32[256,32]{0,1:T(8,128)S(1)}, u32[]{:S(2)}, u32[]{:S(2)}) collective-permute-start(f32[256,32]{0,1:T(8,128)S(1)} %bitcast.73), channel_id=1, source_target_pairs={{0,1},{1,2},{2,3},{3,4},{4,5},{5,6},{6,7},{7,8},{8,9},{9,10},{10,1... | collective-permute-start | bytes 98312 | tf_op jit(solution)/shard_map/ppermute | solution.py:17
  90.2 0.1 fusion.41
  90.3 0.2 fusion.39
  90.5 0.2 collective-permute-done
  90.8 1.2 collective-permute-done.1
  92.0 0.3 fusion.26
  92.3 0.2 copy.55
  92.5 0.8 constant_dynamic-update-slice_fusion
  93.3 1.6 dynamic-update-slice.1
  94.9 1.1 reduce-precision_convert_fusion.1
  96.0 8.8 %fusion = f32[3072,99]{0,1:T(8,128)S(1)} fusion(s32[3072]{0:T(1024)} %copy-done.7, bf16[3072,33]{0,1:T(8,128)(2,1)S(1)} %get-tuple-element.13, bf16[3072,33]{0,1:T(8,128)(2,1)S(1)} %get-tuple-element.14, bf16[3072,33]{0,1:T(8,128)(2,1)S(1)} %get-tuple-element.12), kind=kOutput, calls=%fused_computation.1 | convolution fusion | flops 1879824384 | bytes 1837056 | tf_op jit(solution)/shard_map/dot_general | solution.py:454
  104.8 0.9 slice_add_fusion
  105.7 2.7 copy.45
  108.3 3.8 %all_to_all.17 = f32[16,1,6336]{2,1,0:T(1,128)} reshape(f32[3072,33]{1,0:T(8,128)} %copy.45) | data formatting | bytes 811008 | tf_op jit(solution)/shard_map/all_to_all | solution.py:456
  112.2 24.8 %all_to_all.20 = f32[16,1,6336]{2,1,0:T(1,128)} all-to-all(f32[16,1,6336]{2,1,0:T(1,128)} %all_to_all.17), channel_id=1, replica_groups=mesh['gene'=8,'bin'=16] {'bin'}, dimensions={0} | all-to-all | bytes 811008 | tf_op jit(solution)/shard_map/all_to_all | solution.py:456
  137.0 2.7 reduce.2
  139.7 4.0 %reshape.130 = f32[3072,33]{1,0:T(8,128)} reshape(f32[16,6336]{1,0:T(8,128)} %reduce.2) | data formatting | bytes 811008 | tf_op jit(solution)/shard_map/reshape | solution.py:458
  143.7 2.6 copy.54
  146.3 2.3 fusion.7
  148.6 0.0 reduce-scatter.2.cloned.1.call-done
  148.6 4.8 %fusion.6.x_ref = f32[32,3072]{1,0:T(8,128)} fusion(f32[3072,256]{1,0:T(8,128)S(1)} %copy-done, f32[32,3328]{1,0:T(8,128)} %bitcast.75, f32[3072,32]{0,1:T(8,128)S(1)} %copy.50, f32[3072,32]{0,1:T(8,128)} %copy.54, f32[3072]{0:T(1024)S(1)} %fusion.7), kind=kOutput, calls=%fused_computation.8 | convolution fusion | flops 302579712 | bytes 4763648 | tf_op jit(solution)/shard_map/dot_general | solution.py:484
  153.4 41.5 %shard_map.68 = (f32[8,32,3072]{2,1,0:T(8,128)}, bf16[8,32,3072]{2,1,0:T(8,128)(2,1)}) custom-call(f32[32,3072]{1,0:T(8,128)} %fusion.6.x_ref), custom_call_target="tpu_custom_call" | custom-call | tf_op jit(solution)/shard_map/pallas_call | solution.py:294
  194.9 3.5 %copy.48 = f32[256,3072]{0,1:T(8,128)} copy(f32[256,3072]{1,0:T(8,128)} %bitcast.68) | data formatting | bytes 6291456 | tf_op jit(solution)/shard_map/reshape | solution.py:489
  198.4 10.8 %fusion.4.cross_ref = f32[16,16,2304]{2,1,0:T(8,128)} fusion(bf16[16,16,3072]{2,1,0:T(8,128)(2,1)} %bitcast.64, bf16[3072,2304]{1,0:T(8,128)(2,1)} %param.5), kind=kOutput, calls=%fused_computation.5 | convolution fusion | flops 3623878656 | bytes 18087936 | tf_op jit(solution)/shard_map/dot_general | solution.py:491
  209.3 1.3 fusion.45.gram_ref
  210.6 66.9 %shard_map.69 = f32[16,16,2304]{2,1,0:T(8,128)} custom-call(f32[16,16,2304]{2,1,0:T(8,128)} %fusion.4.cross_ref, f32[16,16,256]{2,1,0:T(8,128)} %fusion.45.gram_ref, f32[256,2304]{1,0:T(8,128)} %load_ref.1), custom_call_target="tpu_custom_call" | custom-call | tf_op jit(solution)/shard_map/pallas_call | solution.py:393
  277.5 3.2 %copy.63 = f32[256,2304]{1,0:T(8,128)} copy(f32[256,2304]{1,0:T(8,128)} %bitcast.63) | data formatting | bytes 4718592
  (17 shorter events, 0.1 us)
Async XLA Ops:
  7.2 11.4 %copy-start = (f32[3072,256]{1,0:T(8,128)S(1)}, f32[3072,256]{1,0:T(8,128)}, u32[]{:S(2)}) copy-start(f32[3072,256]{1,0:T(8,128)} %param.6) | copy-start | bytes 9437188
  8.1 0.6 copy-start.4
  9.2 48.8 %collective-permute-start.2 = (f32[256]{0:T(256)}, f32[256]{0:T(256)}, u32[]{:S(2)}, u32[]{:S(2)}) collective-permute-start(f32[256]{0:T(256)} %bitcast.7), channel_id=1, source_target_pairs={{1,0},{2,1},{3,2},{4,3},{5,4},{6,5},{7,6},{8,7},{9,8},{10,9},{11,1... | collective-permute-start | bytes 3080 | tf_op jit(solution)/shard_map/ppermute | solution.py:17
  12.6 45.5 %collective-permute-start.3 = (f32[256]{0:T(256)}, f32[256]{0:T(256)}, u32[]{:S(2)}, u32[]{:S(2)}) collective-permute-start(f32[256]{0:T(256)} %bitcast.9), channel_id=1, source_target_pairs={{0,1},{1,2},{2,3},{3,4},{4,5},{5,6},{6,7},{7,8},{8,9},{9,10},{10,1... | collective-permute-start | bytes 3080 | tf_op jit(solution)/shard_map/ppermute | solution.py:17
  30.0 29.5 %all-to-all-start = ((f32[16,1,6336]{2,1,0:T(1,128)}), f32[16,1,6336]{2,1,0:T(1,128)}, u32[]{:S(2)}, u32[]{:S(2)}) async-start(f32[16,1,6336]{2,1,0:T(1,128)} %all_to_all.16), calls=%async_computation.1 | async-start | bytes 819200 | tf_op jit(solution)/shard_map/all_to_all | solution.py:430
  38.6 110.0 %reduce-scatter.2.cloned.1.call-start = ((), (), s32[]{:S(2)}) async-start(), calls=%async_computation.3 | async-start | bytes 3833856 | tf_op jit(solution)/shard_map/reduce_scatter | solution.py:475
  39.1 3.1 %copy-start.1 = (f32[256,2304]{1,0:T(8,128)S(1)}, f32[256,2304]{1,0:T(8,128)}, u32[]{:S(2)}) copy-start(f32[256,2304]{1,0:T(8,128)} %load_ref.1) | copy-start | bytes 7077892
  69.1 2.4 copy-start.3
  71.4 7.8 %copy-start.7 = (s32[3072]{0:T(1024)}, s32[3072]{0:T(1024)S(1)}, u32[]{:S(2)}) copy-start(s32[3072]{0:T(1024)S(1)} %fusion.9) | copy-start | bytes 36868
  79.3 2.7 copy-start.5
  83.1 7.6 %collective-permute-start = (f32[256,32]{0,1:T(8,128)S(1)}, f32[256,32]{0,1:T(8,128)S(1)}, u32[]{:S(2)}, u32[]{:S(2)}) collective-permute-start(f32[256,32]{0,1:T(8,128)S(1)} %bitcast.74), channel_id=1, source_target_pairs={{1,0},{2,1},{3,2},{4,3},{5,4},{6,5},{7,6},{8,7},{9,8},{10,9},{11,1... | collective-permute-start | bytes 98312 | tf_op jit(solution)/shard_map/ppermute | solution.py:17
  85.2 6.7 %collective-permute-start.1 = (f32[256,32]{0,1:T(8,128)S(1)}, f32[256,32]{0,1:T(8,128)S(1)}, u32[]{:S(2)}, u32[]{:S(2)}) collective-permute-start(f32[256,32]{0,1:T(8,128)S(1)} %bitcast.73), channel_id=1, source_target_pairs={{0,1},{1,2},{2,3},{3,4},{4,5},{5,6},{6,7},{7,8},{8,9},{9,10},{10,1... | collective-permute-start | bytes 98312 | tf_op jit(solution)/shard_map/ppermute | solution.py:17
  92.3 1.0 copy-start.6
  198.4 10.8 %copy-start.2 = (bf16[8,32,3072]{2,1,0:T(8,128)(2,1)S(1)}, bf16[8,32,3072]{2,1,0:T(8,128)(2,1)}, u32[]{:S(2)}) copy-start(bf16[8,32,3072]{2,1,0:T(8,128)(2,1)} %get-tuple-element.5) | copy-start | bytes 4718596
Sparse Core Ops, SparseCore 0:
  56.9 82.3 reduce-scatter.1

commit v2 on v1

--- a/solution.py
+++ b/solution.py
@@ -428,7 +428,7 @@
     grid_rows, grid_cols = edge_codes.shape
     payload = jnp.concatenate([own, position.astype(jnp.float32)[:, None]], 1)
     got = lax.all_to_all(
-        payload.reshape(bin_count, group_size * (width + 1)), "bin", 0, 0, tiled=True
+        payload.reshape(bin_count, group_size, width + 1), "bin", 0, 0, tiled=True
     ).reshape(row_count, width + 1)
     tile_slot = got[:, width].astype(jnp.int32) - lax.axis_index("bin") * row_count
     cells = lax.broadcasted_iota(jnp.int32, (row_count, row_count), 1)
@@ -454,7 +454,7 @@
         jnp.dot(onehot, split_three(back), preferred_element_type=jnp.float32), width + 1
     )
     ret = lax.all_to_all(
-        back_rows.reshape(bin_count, group_size * (width + 1)), "bin", 0, 0, tiled=True
+        back_rows.reshape(bin_count, group_size, width + 1), "bin", 0, 0, tiled=True
     ).reshape(row_count, width + 1)
     return (ret[:, :width], ret[:, width])
 

time: 292 us -> 279 us (0.955); the launches traced: 288 us -> 278 us
  local copies, waits for them, and re-layouts: 44.6 us -> 31.7 us
  other arithmetic: 22.9 us -> 14.5 us
  waiting for transfers between devices: 1.42 us -> 7.65 us
  blocking collectives: 24.8 us -> 29.2 us
  Pallas kernels: 108 us -> 111 us
    reduce_scatter x1, waiting for transfers between devices: 0.02 us -> 6.44 us  [on_device(): lax.psum_scatter(both.reshape(gene_count, width, -1), 'gene', scatter_dim...]
    all_to_all x2 -> x0, other arithmetic: 5.45 us -> none  [the longest x1 2.73 us: stencil_term(): lax.all_to_all(payload.reshape(bin_count, group_size * (width + 1)), 'bin...]
    unnamed x25 -> x21, local copies, waits for them, and re-layouts: 12.8 us -> 7.35 us
    all_to_all x2, local copies, waits for them, and re-layouts: 7.69 us -> 3.03 us  [the longest x1 2.06 us: stencil_term(): lax.all_to_all(payload.reshape(bin_count, group_size, width + 1), 'bin',...]
    all_to_all x1, blocking collectives: 24.8 us -> 29.2 us  [stencil_term(): lax.all_to_all(back_rows.reshape(bin_count, group_size, width + 1), 'bin'...]
    reshape x2 -> x4, local copies, waits for them, and re-layouts: 7.94 us -> 7.55 us  [the longest x2 3.44 us: stencil_term(): back_rows.reshape(bin_count, group_size, width + 1)]
  transfers between devices with their start and end apart: 6 -> 6, of which waited for: 2 -> 3; matrix products, arithmetic and copies ran while one was open for 28% -> 24% of each run, Pallas kernels for 0% -> 0%
where the time goes in v2:
time: 279 us; the launch traced here: 278 us
  Pallas kernels  111 us (40%)
  matrix products  46.2 us (17%)
  local copies, waits for them, and re-layouts  31.7 us (11%)
  blocking collectives  29.2 us (10%)
  starting transfers between devices  23.8 us (9%)
  other arithmetic  14.5 us (5%)
  between operations  14.3 us (5%)
  waiting for transfers between devices  7.65 us (3%)
    pallas_call x1, Pallas kernels, loadings_update(): pl.pallas_call(functools.partial(loadings_kernel, count), out_shape=jax.S...  69.1 us
    pallas_call x1, Pallas kernels, factor_gather(): pl.pallas_call(functools.partial(factor_gather_kernel, count), out_shape=...  41.7 us
    all_to_all x1, blocking collectives, stencil_term(): lax.all_to_all(back_rows.reshape(bin_count, group_size, width + 1), 'bin'...  29.2 us
    ppermute x4, starting transfers between devices, passed_along(): return lax.ppermute(block, axis, route)  15.2 us
    dot_general x1, matrix products, on_device(): cross_part = jnp.dot(fac_bf_t, counts, preferred_element_type=jnp.float32)  10.8 us
    dot_general x1, matrix products, on_device(): lax.dot_general(load_bf, counts, right_dims, preferred_element_type=jnp.f...  10.7 us
    all_to_all x1, starting transfers between devices, stencil_term(): lax.all_to_all(payload.reshape(bin_count, group_size, width + 1), 'bin',...  8.57 us
    dot_general x1, matrix products, stencil_term(): jnp.dot(onehot, split_three(back), preferred_element_type=jnp.float32)  8.05 us
  transfers between devices with their start and end apart: 6, of which 3 were waited for; matrix products, arithmetic and copies ran while one was open for 24% of the time, Pallas kernels for 0%

profile of v2, /device:TPU:1, one launch (start us, length us, event | category | flops | bytes accessed | tf_op | source)
XLA Modules:
  0.0 278.1 jit_solution(9884688852218795289)
XLA Ops:
  7.2 0.0 copy-start
  7.2 0.9 fusion.38
  8.1 0.6 copy-done.3
  8.7 0.6 fusion.43
  9.2 3.3 %collective-permute-start.2 = (f32[256]{0:T(256)}, f32[256]{0:T(256)}, u32[]{:S(2)}, u32[]{:S(2)}) collective-permute-start(f32[256]{0:T(256)} %bitcast.7), channel_id=1, source_target_pairs={{1,0},{2,1},{3,2},{4,3},{5,4},{6,5},{7,6},{8,7},{9,8},{10,9},{11,1... | collective-permute-start | bytes 3080 | tf_op jit(solution)/shard_map/ppermute | solution.py:17
  12.6 4.6 %collective-permute-start.3 = (f32[256]{0:T(256)}, f32[256]{0:T(256)}, u32[]{:S(2)}, u32[]{:S(2)}) collective-permute-start(f32[256]{0:T(256)} %bitcast.9), channel_id=1, source_target_pairs={{0,1},{1,2},{2,3},{3,4},{4,5},{5,6},{6,7},{7,8},{8,9},{9,10},{10,1... | collective-permute-start | bytes 3080 | tf_op jit(solution)/shard_map/ppermute | solution.py:17
  17.2 0.7 convert_element_type.25
  17.9 0.7 concatenate.56
  18.6 0.0 copy-done
  18.6 1.6 constant_dynamic-slice_fusion
  20.2 1.8 copy.34
  22.1 1.0 concatenate.55
  23.1 1.1 pad_maximum_fusion.1
  24.2 1.2 copy.26
  25.4 8.6 %all-to-all-start = ((f32[16,192,33]{1,2,0:T(8,128)}), f32[16,192,33]{1,2,0:T(8,128)}, u32[]{:S(2)}, u32[]{:S(2)}) async-start(f32[16,192,33]{1,2,0:T(8,128)} %copy.26), calls=%async_computation.1 | async-start | bytes 1310720 | tf_op jit(solution)/shard_map/all_to_all | solution.py:430
  33.9 0.0 reduce-scatter.2.cloned.1.call-start
  34.0 0.0 copy-start.1
  34.0 3.0 %fusion.17 = f32[256,256]{1,0:T(8,128)S(1)} fusion(f32[256,2304]{1,0:T(8,128)} %load_ref.1), kind=kOutput, calls=%fused_computation.24 | convolution fusion | flops 302579712 | bytes 2621440 | tf_op jit(solution)/shard_map/dot_general | solution.py:473
  37.0 0.0 copy-done.1
  37.1 10.7 %fusion.19 = f32[256,3072]{1,0:T(8,128)} fusion(bf16[3072,2304]{1,0:T(8,128)(2,1)} %param.5, f32[256,2304]{1,0:T(8,128)S(1)} %copy-done.1), kind=kOutput, calls=%fused_computation.26 | convolution fusion | flops 3624468480 | bytes 19660800 | tf_op jit(solution)/shard_map/dot_general | solution.py:472
  47.7 3.8 %pad_maximum_fusion = f32[256,3328]{1,0:T(8,128)} fusion(f32[256,256]{1,0:T(8,128)S(1)} %fusion.17, f32[256,3072]{1,0:T(8,128)} %fusion.19), kind=kLoop, calls=%fused_computation.9 | loop fusion | flops 851968 | bytes 6815744 | tf_op jit(solution)/shard_map/concatenate | solution.py:474
  51.6 0.0 reduce-scatter.2.cloned.1.call-update
  51.6 0.6 fusion.44
  52.2 0.7 fusion.42
  52.9 0.0 collective-permute-done.2
  52.9 0.0 collective-permute-done.3
  52.9 0.9 fusion.34
  53.8 0.6 copy.38
  54.4 0.0 all-to-all-done
  54.4 2.1 copy.27
  56.4 2.1 reshape.123
  58.5 0.9 fusion.35
  59.4 1.1 reduce-precision_convert_fusion.3
  60.5 7.5 %fusion.1 = f32[3072,96]{0,1:T(8,128)S(1)} fusion(s32[3072]{0:T(1024)S(1)} %bitcast.86, bf16[3072,32]{0,1:T(8,128)(2,1)S(1)} %get-tuple-element.16, bf16[3072,32]{0,1:T(8,128)(2,1)S(1)} %get-tuple-element.17, bf16[3072,32]{0,1:T(8,128)(2,1)S(1)} %get-tuple-element.15), kind=kOutput, calls=%fused_computation.2 | convolution fusion | flops 1823145984 | bytes 1781760 | tf_op jit(solution)/shard_map/dot_general | solution.py:436
  68.1 0.8 slice_add_fusion.2
  68.9 1.9 reshape.124
  70.8 1.1 broadcast_multiply_fusion
  71.9 2.1 collective-permute-start
  74.0 5.2 %collective-permute-start.1 = (f32[256,32]{0,1:T(8,128)S(1)}, f32[256,32]{0,1:T(8,128)S(1)}, u32[]{:S(2)}, u32[]{:S(2)}) collective-permute-start(f32[256,32]{0,1:T(8,128)S(1)} %bitcast.84), channel_id=1, source_target_pairs={{0,1},{1,2},{2,3},{3,4},{4,5},{5,6},{6,7},{7,8},{8,9},{9,10},{10,1... | collective-permute-start | bytes 98312 | tf_op jit(solution)/shard_map/ppermute | solution.py:17
  79.2 0.1 fusion.41
  79.3 0.2 fusion.39
  79.5 0.4 collective-permute-done
  80.0 0.8 collective-permute-done.1
  80.7 0.3 fusion.23
  81.1 0.2 copy.37
  81.3 0.8 constant_dynamic-update-slice_fusion
  82.1 1.6 dynamic-update-slice.1
  83.6 1.1 reduce-precision_convert_fusion.1
  84.8 8.1 %fusion = f32[3072,99]{0,1:T(8,128)S(1)} fusion(s32[3072]{0:T(1024)S(1)} %bitcast.87, bf16[3072,33]{0,1:T(8,128)(2,1)S(1)} %get-tuple-element.13, bf16[3072,33]{0,1:T(8,128)(2,1)S(1)} %get-tuple-element.14, bf16[3072,33]{0,1:T(8,128)(2,1)S(1)} %get-tuple-element.12), kind=kOutput, calls=%fused_computation.1 | convolution fusion | flops 1879824384 | bytes 1837056 | tf_op jit(solution)/shard_map/dot_general | solution.py:454
  92.9 0.9 slice_add_fusion
  93.8 2.1 reshape.127
  95.8 1.4 copy.30
  97.2 29.2 %all_to_all.10 = f32[16,192,33]{1,2,0:T(8,128)S(1)} all-to-all(f32[16,192,33]{1,2,0:T(8,128)S(1)} %copy.30), channel_id=1, replica_groups=mesh['gene'=8,'bin'=16] {'bin'}, dimensions={0} | all-to-all | bytes 811008 | tf_op jit(solution)/shard_map/all_to_all | solution.py:456
  126.4 1.0 copy.31
  127.4 2.1 reshape.128
  129.4 0.9 slice_multiply_fusion.1
  130.3 6.4 %reduce-scatter.2.cloned.1.call-done = f32[1,32,3328]{2,1,0:T(8,128)} async-done(((f32[8,32,3328]{2,1,0:T(8,128)}), f32[1,32,3328]{2,1,0:T(8,128)}) %reduce-scatter.2.cloned.1.call-update) | async-done | bytes 426000 | tf_op jit(solution)/shard_map/reduce_scatter | solution.py:475
  136.8 4.8 %fusion.6.x_ref = f32[32,3072]{1,0:T(8,128)} fusion(f32[3072,256]{1,0:T(8,128)S(1)} %copy-done, f32[3072,33]{0,1:T(8,128)} %reshape.128, f32[32,3328]{1,0:T(8,128)} %bitcast.88, f32[3072,32]{0,1:T(8,128)S(1)} %copy.34, f32[3072]{0:T(1024)S(1)} %bitcast.82), kind=kOutput, calls=%fused_computation.8 | convolution fusion | flops 302579712 | bytes 4763648 | tf_op jit(solution)/shard_map/dot_general | solution.py:484
  141.6 41.7 %shard_map.68 = (f32[8,32,3072]{2,1,0:T(8,128)}, bf16[8,32,3072]{2,1,0:T(8,128)(2,1)}) custom-call(f32[32,3072]{1,0:T(8,128)} %fusion.6.x_ref), custom_call_target="tpu_custom_call" | custom-call | tf_op jit(solution)/shard_map/pallas_call | solution.py:294
  183.3 3.5 %copy.32 = f32[256,3072]{0,1:T(8,128)} copy(f32[256,3072]{1,0:T(8,128)} %bitcast.79) | data formatting | bytes 6291456 | tf_op jit(solution)/shard_map/reshape | solution.py:489
  186.8 10.8 %fusion.4.cross_ref = f32[16,16,2304]{2,1,0:T(8,128)} fusion(bf16[16,16,3072]{2,1,0:T(8,128)(2,1)} %bitcast.75, bf16[3072,2304]{1,0:T(8,128)(2,1)} %param.5), kind=kOutput, calls=%fused_computation.5 | convolution fusion | flops 3623878656 | bytes 18087936 | tf_op jit(solution)/shard_map/dot_general | solution.py:491
  197.7 1.3 fusion.45.gram_ref
  199.0 69.1 %shard_map.69 = f32[16,16,2304]{2,1,0:T(8,128)} custom-call(f32[16,16,2304]{2,1,0:T(8,128)} %fusion.4.cross_ref, f32[16,16,256]{2,1,0:T(8,128)} %fusion.45.gram_ref, f32[256,2304]{1,0:T(8,128)} %load_ref.1), custom_call_target="tpu_custom_call" | custom-call | tf_op jit(solution)/shard_map/pallas_call | solution.py:393
  268.1 3.2 %copy.45 = f32[256,2304]{1,0:T(8,128)} copy(f32[256,2304]{1,0:T(8,128)} %bitcast.74) | data formatting | bytes 4718592
  (14 shorter events, 0.1 us)
Async XLA Ops:
  7.2 11.4 %copy-start = (f32[3072,256]{1,0:T(8,128)S(1)}, f32[3072,256]{1,0:T(8,128)}, u32[]{:S(2)}) copy-start(f32[3072,256]{1,0:T(8,128)} %param.6) | copy-start | bytes 9437188
  8.1 0.6 copy-start.3
  9.2 43.7 %collective-permute-start.2 = (f32[256]{0:T(256)}, f32[256]{0:T(256)}, u32[]{:S(2)}, u32[]{:S(2)}) collective-permute-start(f32[256]{0:T(256)} %bitcast.7), channel_id=1, source_target_pairs={{1,0},{2,1},{3,2},{4,3},{5,4},{6,5},{7,6},{8,7},{9,8},{10,9},{11,1... | collective-permute-start | bytes 3080 | tf_op jit(solution)/shard_map/ppermute | solution.py:17
  12.6 40.3 %collective-permute-start.3 = (f32[256]{0:T(256)}, f32[256]{0:T(256)}, u32[]{:S(2)}, u32[]{:S(2)}) collective-permute-start(f32[256]{0:T(256)} %bitcast.9), channel_id=1, source_target_pairs={{0,1},{1,2},{2,3},{3,4},{4,5},{5,6},{6,7},{7,8},{8,9},{9,10},{10,1... | collective-permute-start | bytes 3080 | tf_op jit(solution)/shard_map/ppermute | solution.py:17
  25.4 29.0 %all-to-all-start = ((f32[16,192,33]{1,2,0:T(8,128)}), f32[16,192,33]{1,2,0:T(8,128)}, u32[]{:S(2)}, u32[]{:S(2)}) async-start(f32[16,192,33]{1,2,0:T(8,128)} %copy.26), calls=%async_computation.1 | async-start | bytes 1310720 | tf_op jit(solution)/shard_map/all_to_all | solution.py:430
  33.9 102.8 %reduce-scatter.2.cloned.1.call-start = ((), (), s32[]{:S(2)}) async-start(), calls=%async_computation.3 | async-start | bytes 3833856 | tf_op jit(solution)/shard_map/reduce_scatter | solution.py:475
  34.0 3.1 %copy-start.1 = (f32[256,2304]{1,0:T(8,128)S(1)}, f32[256,2304]{1,0:T(8,128)}, u32[]{:S(2)}) copy-start(f32[256,2304]{1,0:T(8,128)} %load_ref.1) | copy-start | bytes 7077892
  59.4 8.6 %copy-start.5 = (s32[3072,1]{0,1:T(1,128)}, s32[3072,1]{0,1:T(1,128)S(1)}, u32[]{:S(2)}) copy-start(s32[3072,1]{0,1:T(1,128)S(1)} %fusion.35) | copy-start | bytes 36868
  68.1 2.7 copy-start.4
  71.9 8.0 %collective-permute-start = (f32[256,32]{0,1:T(8,128)S(1)}, f32[256,32]{0,1:T(8,128)S(1)}, u32[]{:S(2)}, u32[]{:S(2)}) collective-permute-start(f32[256,32]{0,1:T(8,128)S(1)} %bitcast.85), channel_id=1, source_target_pairs={{1,0},{2,1},{3,2},{4,3},{5,4},{6,5},{7,6},{8,7},{9,8},{10,9},{11,1... | collective-permute-start | bytes 98312 | tf_op jit(solution)/shard_map/ppermute | solution.py:17
  74.0 6.7 %collective-permute-start.1 = (f32[256,32]{0,1:T(8,128)S(1)}, f32[256,32]{0,1:T(8,128)S(1)}, u32[]{:S(2)}, u32[]{:S(2)}) collective-permute-start(f32[256,32]{0,1:T(8,128)S(1)} %bitcast.84), channel_id=1, source_target_pairs={{0,1},{1,2},{2,3},{3,4},{4,5},{5,6},{6,7},{7,8},{8,9},{9,10},{10,1... | collective-permute-start | bytes 98312 | tf_op jit(solution)/shard_map/ppermute | solution.py:17
  81.1 3.8 %copy-start.6 = (s32[3072,1]{0,1:T(1,128)S(1)}, s32[3072,1]{0,1:T(1,128)}, u32[]{:S(2)}) copy-start(s32[3072,1]{0,1:T(1,128)} %copy-done.5) | copy-start | bytes 36868
  186.8 10.8 %copy-start.2 = (bf16[8,32,3072]{2,1,0:T(8,128)(2,1)S(1)}, bf16[8,32,3072]{2,1,0:T(8,128)(2,1)}, u32[]{:S(2)}) copy-start(bf16[8,32,3072]{2,1,0:T(8,128)(2,1)} %get-tuple-element.5) | copy-start | bytes 4718596
Sparse Core Ops, SparseCore 0:
  51.7 85.0 reduce-scatter.1
